TPU v7x, 256 devices: a whole 4x4x8 slice. The times are simulated.
256 devices in a mesh: wide: 128 (over x, y, z_lo, core), head: 2 (over z_hi).
Axes of the slice: x: 4, y: 4, z: 8 (z_hi: 2, z_lo: 4; z = z_hi * 4 + z_lo), core: 2. Of those that a mesh axis runs over, the one named last changes fastest.
Arguments:
- branch_query: bfloat16 [512, 8192], P('wide', 'head'), may hold values from -6 to 6
- key_new: bfloat16 [512, 1024], P('wide', 'head'), may hold values from -6 to 6
- value_new: bfloat16 [512, 1024], P('wide', 'head'), may hold values from -6 to 6
- pool_pages: bfloat16 [2, 8192, 16, 1024], P(None, 'wide', None, 'head'), may hold values from -6 to 6
- page_table: int32 [512, 16], P('wide'), may hold values from 0 to 63, as said below
- tail_length: int32 [512], P('wide'), may hold values from 1 to 256
- parent_row: int32 [512], P('wide'), may hold values from 0 to 511, as said below
- residual: bfloat16 [512, 8192], P(('wide', 'head')), may hold values from -6 to 6
- norm_gain: float32 [8192], replicated, may hold values from 0.5 to 1.5
- gate_blocks: bfloat16 [128, 32, 128, 128], P('wide'), may hold values from -0.09375 to 0.09375
- up_blocks: bfloat16 [128, 32, 128, 128], P('wide'), may hold values from -0.09375 to 0.09375
- gate_up_keep: int32 [128, 32], P('wide'), may hold values from 0 to 63, as said below
- gate_scale: float32 [128, 32], P('wide'), may hold values from 0.5 to 2
- up_scale: float32 [128, 32], P('wide'), may hold values from 0.5 to 2
- down_blocks: bfloat16 [128, 32, 128, 128], P('wide'), may hold values from -0.0625 to 0.0625
- down_keep: int32 [128, 32], P('wide'), may hold values from 0 to 63, as said below
- down_scale: float32 [128, 32], P('wide'), may hold values from 0.5 to 2
Outputs:
- layer_out: bfloat16 [512, 8192], P(('wide', 'head'))
Inputs may be any that keep to these rules, and one draw needn't show every extreme that they name: parent_row never falls with the branch index, and parent_row[b] <= b and parent_row[b] > b - 4. `page_table`: the entries of the 4 rows held by one index of wide name each of that index's 64 pages once. `gate_up_keep`: each row names 32 different blocks. `down_keep`: each row names 32 different blocks.
All inputs are finite; a program needn't handle non-finite values.
Results may differ from a plain program's by a relative error of at most 0.017.
Values may be sent and summed in bfloat16 or wider, within the bound.
A program may use at most 64 MiB of HBM per device.

v0:
```python
import math
import jax
import jax.numpy as jnp
from jax import lax
from jax.sharding import PartitionSpec as P

HD = 128
BLK = 128


def shifted(block, axis, distance):
    devices = range(lax.axis_size(axis))
    route = [(i - distance, i) for i in devices if i - distance in devices]
    return lax.ppermute(block, axis, route)


def attend(branch_query, key_new, value_new, child_tails, child_length):
    row_count = branch_query.shape[0]
    groups = key_new.shape[1] // HD
    per_group = branch_query.shape[1] // (groups * HD)
    tail_size = child_tails.shape[2]
    queries = branch_query.reshape(row_count, groups, per_group, HD)
    tail_keys = child_tails[0].reshape(row_count, tail_size, groups, HD)
    tail_values = child_tails[1].reshape(row_count, tail_size, groups, HD)
    own_keys = key_new.reshape(row_count, groups, HD)
    own_values = value_new.reshape(row_count, groups, HD)
    factor = 1.0 / math.sqrt(HD)
    tail_scores = (
        jnp.einsum("rgjd,rtgd->rgjt", queries, tail_keys, preferred_element_type=jnp.float32)
        * factor
    )
    own_scores = (
        jnp.einsum("rgjd,rgd->rgj", queries, own_keys, preferred_element_type=jnp.float32) * factor
    )
    live_mask = (jnp.arange(tail_size, dtype=jnp.float32)[None, :] < child_length[:, None])[
        :, None, None, :
    ]
    top_score = jnp.maximum(jnp.max(jnp.where(live_mask, tail_scores, -1e30), axis=-1), own_scores)
    tail_exp = jnp.where(live_mask, jnp.exp(tail_scores - top_score[..., None]), 0.0)
    own_exp = jnp.exp(own_scores - top_score)
    totals = jnp.sum(tail_exp, axis=-1) + own_exp
    tail_weights = (tail_exp / totals[..., None]).astype(jnp.bfloat16)
    own_weights = (own_exp / totals).astype(jnp.bfloat16)
    mixture = jnp.einsum(
        "rgjt,rtgd->rgjd", tail_weights, tail_values, preferred_element_type=jnp.float32
    )
    mixture = mixture + own_weights[..., None].astype(jnp.float32) * own_values[
        :, :, None, :
    ].astype(jnp.float32)
    return mixture.reshape(row_count, -1).astype(jnp.bfloat16)


def ffn_terms(
    rows_in, gate_blocks, up_blocks, gate_up_keep, gate_scale, up_scale, down_blocks, down_scale
):
    row_count = rows_in.shape[0]
    blocks = rows_in.reshape(row_count, -1, BLK)
    picked = blocks[:, gate_up_keep]
    gate_part = jnp.einsum(
        "rckd,ckdf->rckf", picked, gate_blocks, preferred_element_type=jnp.float32
    )
    up_part = jnp.einsum("rckd,ckdf->rckf", picked, up_blocks, preferred_element_type=jnp.float32)
    gate_sum = jnp.sum(gate_part * gate_scale[None, :, :, None], axis=2)
    up_sum = jnp.sum(up_part * up_scale[None, :, :, None], axis=2)
    hidden = (jax.nn.silu(gate_sum) * up_sum).astype(jnp.bfloat16)
    contrib = (
        jnp.einsum("rcf,ckfe->rcke", hidden, down_blocks, preferred_element_type=jnp.float32)
        * down_scale[None, :, :, None]
    )
    return contrib.reshape(row_count, -1, BLK)


def feed_forward(
    rows_in,
    gate_blocks,
    up_blocks,
    gate_up_keep,
    gate_scale,
    up_scale,
    down_blocks,
    down_keep,
    down_scale,
):
    row_count = rows_in.shape[0]
    contrib = ffn_terms(
        rows_in, gate_blocks, up_blocks, gate_up_keep, gate_scale, up_scale, down_blocks, down_scale
    )
    placed = jnp.zeros((row_count, rows_in.shape[1] // BLK, BLK), jnp.float32)
    placed = placed.at[:, down_keep.reshape(-1)].add(contrib)
    return placed.reshape(row_count, -1)


def per_device(
    branch_query,
    key_new,
    value_new,
    pool_pages,
    page_table,
    tail_length,
    parent_row,
    residual,
    norm_gain,
    gate_blocks,
    up_blocks,
    gate_up_keep,
    gate_scale,
    up_scale,
    down_blocks,
    down_keep,
    down_scale,
):
    row_count = branch_query.shape[0]
    tail_size = page_table.shape[1] * pool_pages.shape[2]
    own_tails = pool_pages[:, page_table].reshape(2, row_count, tail_size, pool_pages.shape[3])
    own_length = tail_length.astype(jnp.bfloat16)
    prior_tails, prior_length = shifted((own_tails, own_length), "wide", 1)
    both_tails = jnp.concatenate([prior_tails, own_tails], axis=1)
    both_length = jnp.concatenate([prior_length, own_length]).astype(jnp.float32)
    local_parent = parent_row - (lax.axis_index("wide") - 1) * row_count
    child_tails = both_tails[:, local_parent]
    child_length = both_length[local_parent]
    attention = attend(branch_query, key_new, value_new, child_tails, child_length)
    head_rows = lax.all_to_all(attention, "head", split_axis=0, concat_axis=1, tiled=True)
    middle = residual.astype(jnp.float32) + head_rows.astype(jnp.float32)
    normed = (
        middle * lax.rsqrt(jnp.mean(middle * middle, axis=-1, keepdims=True) + 1e-05) * norm_gain
    ).astype(jnp.bfloat16)
    gathered = lax.all_gather(normed, "wide", axis=0, tiled=True)
    ffn_share = lax.psum_scatter(
        feed_forward(
            gathered,
            gate_blocks,
            up_blocks,
            gate_up_keep,
            gate_scale,
            up_scale,
            down_blocks,
            down_keep,
            down_scale,
        ),
        "wide",
        scatter_dimension=0,
        tiled=True,
    )
    return (middle + ffn_share).astype(jnp.bfloat16)


def solution(mesh):
    placed = (
        P("wide", "head"),
        P("wide", "head"),
        P("wide", "head"),
        P(None, "wide", None, "head"),
        P("wide", None),
        P("wide"),
        P("wide"),
        P(("wide", "head"), None),
        P(),
        P("wide", None, None, None),
        P("wide", None, None, None),
        P("wide", None),
        P("wide", None),
        P("wide", None),
        P("wide", None, None, None),
        P("wide", None),
        P("wide", None),
    )
    return jax.shard_map(
        per_device, mesh=mesh, in_specs=placed, out_specs=P(("wide", "head"), None), check_vma=False
    )
```

profile of v0, /device:TPU:0, one launch (start us, length us, event | category | flops | bytes accessed | tf_op | source)
XLA Modules:
  0.0 1664.6 jit_solution(4971448282090236320)
XLA Ops:
  6.5 0.8 compare_select_fusion
  7.5 0.7 copy-done
  8.2 2.0 gather_fusion.1
  10.2 3.1 copy.39
  13.3 2.6 collective-permute-start.1
  16.0 1.5 collective-permute-start
  17.7 0.7 collective-permute-done
  18.5 0.6 gather_fusion
  19.2 4.5 pad_maximum_fusion
  23.7 2.9 gather_fusion.2
  26.6 1.2 fusion.33
  27.7 1.5 copy.40
  29.8 0.5 copy.42
  30.4 0.4 fusion.5
  30.8 15.1 all_to_all.10
  46.2 0.7 fusion.24
  47.2 221.7 %all-gather.3.cloned.1.call-done = bf16[128,2,8192]{2,1,0:T(2,128)(2,1)} async-done(((bf16[1,2,8192]{2,1,0:T(2,128)(2,1)}), bf16[128,2,8192]{2,1,0:T(2,128)(2,1)}) %all-gather.3.cloned.1.call-update) | async-done | bytes 4194320 | tf_op jit(solution)/shard_map/all_gather | solution.py:128
  268.9 7.8 reshape.150
  276.7 6.9 copy.44
  283.6 3.2 gather_fusion.3
  286.8 2.1 fusion.1
  288.9 0.7 fusion.2
  289.7 2.7 fusion
  292.3 4.3 broadcast_in_dim.48
  296.6 10.2 scatter_fusion
  306.8 9.0 copy.45
  315.8 0.6 copy-done.16
  316.4 0.6 dynamic-slice
  317.6 1331.2 %all-reduce.3.cloned.1.call-done = f32[256,8192]{0,1:T(8,128)} async-done(((f32[256,8192]{0,1:T(8,128)}), f32[256,8192]{0,1:T(8,128)}) %all-reduce.3.cloned.1.call-update) | async-done | bytes 8388624
  1648.8 5.4 constant_dynamic-slice_fusion
  1654.3 2.8 copy.46
  1657.1 0.7 add_convert_fusion
  (58 shorter events, 1.5 us)
Async XLA Ops:
  6.5 1.6 copy-start
  6.5 262.4 %all-gather.3.cloned.1.call-start = ((), (), s32[]{:S(2)}) async-start(), calls=%async_computation.1 | async-start | bytes 4227072 | tf_op jit(solution)/shard_map/all_gather | solution.py:128
  8.1 7.8 copy-start.10
  8.1 9.3 copy-start.6
  8.1 9.3 copy-start.7
  8.1 9.4 copy-start.11
  8.2 9.4 copy-start.4
  13.3 5.8 collective-permute-start.1
  16.0 2.4 collective-permute-start
  27.7 18.2 %copy-start.3 = (bf16[2,8192]{1,0:T(2,128)(2,1)S(1)}, bf16[2,8192]{1,0:T(2,128)(2,1)}, u32[]{:S(2)}) copy-start(bf16[2,8192]{1,0:T(2,128)(2,1)} %param.24) | copy-start | bytes 98308
  27.7 18.4 %copy-start.5 = (f32[8192]{0:T(1024)S(1)}, f32[8192]{0:T(1024)}, u32[]{:S(2)}) copy-start(f32[8192]{0:T(1024)} %param.25) | copy-start | bytes 98308
  27.7 19.4 %copy-start.12 = (s32[1,32]{1,0:T(1,128)S(1)}, s32[1,32]{1,0:T(1,128)}, u32[]{:S(2)}) copy-start(s32[1,32]{1,0:T(1,128)} %param.28) | copy-start | bytes 388
  27.7 19.4 %copy-start.13 = (s32[1,32]{1,0:T(1,128)S(1)}, s32[1,32]{1,0:T(1,128)}, u32[]{:S(2)}) copy-start(s32[1,32]{1,0:T(1,128)} %param.32) | copy-start | bytes 388
  46.9 1601.9 %all-reduce.3.cloned.1.call-start = ((), (), s32[]{:S(2)}) async-start(), calls=%async_computation.2 | async-start | bytes 16777216
  283.6 3.2 copy-start.14
  283.6 5.3 copy-start.15
  286.8 2.1 copy-start.9
  286.8 2.9 copy-start.2
  286.8 2.8 copy-start.8
  315.7 0.7 copy-start.16
  1648.8 9.0 copy-start.1
Sparse Core Ops, SparseCore 0:
  47.0 221.8 all-gather.2
  315.9 1332.9 all-reduce.2
where the time goes:
time: 1670 us; the launch traced here: 1660 us
  waiting for transfers between devices  1550 us (93%)
  local copies, waits for them, and re-layouts  53.3 us (3%)
  other arithmetic  17.5 us (1%)
    unnamed x3, waiting for transfers between devices  1330 us
    all_gather x1, waiting for transfers between devices, per_device(): gathered = lax.all_gather(normed, 'wide', axis=0, tiled=True)  222 us
  transfers between devices with their start and end apart: 4, of which 3 were waited for; matrix products, arithmetic and copies ran while one was open for 0% of the time, Pallas kernels for 0%

commit v1 on v0

--- a/solution.py
+++ b/solution.py
@@ -125,7 +125,9 @@
     normed = (
         middle * lax.rsqrt(jnp.mean(middle * middle, axis=-1, keepdims=True) + 1e-05) * norm_gain
     ).astype(jnp.bfloat16)
-    gathered = lax.all_gather(normed, "wide", axis=0, tiled=True)
+    gathered = jnp.concatenate(
+        lax.all_to_all(jnp.stack([normed] * lax.axis_size("wide")), "wide", 0, 0), axis=0
+    )
     ffn_share = lax.psum_scatter(
         feed_forward(
             gathered,

time: 1670 us -> 1570 us (0.940)
  waiting for transfers between devices: 1550 us -> 1420 us
  starting transfers between devices: 4.34 us -> 38.7 us
    all_gather x1 -> x0, waiting for transfers between devices: 222 us -> none  [per_device(): gathered = lax.all_gather(normed, 'wide', axis=0, tiled=True)]
    all_to_all x0 -> x1, waiting for transfers between devices: none -> 96.5 us  [per_device(): lax.all_to_all(jnp.stack([normed] * lax.axis_size('wide')), 'wide', 0, 0)]
    all_to_all x0 -> x1, starting transfers between devices: none -> 34.4 us  [per_device(): lax.all_to_all(jnp.stack([normed] * lax.axis_size('wide')), 'wide', 0, 0)]
    another operation x0 -> x3, local copies, waits for them, and re-layouts: none -> 20.9 us  [the longest x2 14.7 us: ffn_terms(): blocks = rows_in.reshape(row_count, -1, BLK)]
    unnamed x3 -> x2, waiting for transfers between devices: 1330 us -> 1330 us
where the time goes in v1:
time: 1570 us
  waiting for transfers between devices  1420 us (90%)
  local copies, waits for them, and re-layouts  59.5 us (4%)
  starting transfers between devices  38.7 us (2%)
  other arithmetic  17 us (1%)
    unnamed x2, waiting for transfers between devices  1330 us
    all_to_all x1, waiting for transfers between devices, per_device(): lax.all_to_all(jnp.stack([normed] * lax.axis_size('wide')), 'wide', 0, 0)  96.5 us
    all_to_all x1, starting transfers between devices, per_device(): lax.all_to_all(jnp.stack([normed] * lax.axis_size('wide')), 'wide', 0, 0)  34.4 us
  transfers between devices with their start and end apart: 4, of which 3 were waited for; matrix products, arithmetic and copies ran while one was open for 0% of the time, Pallas kernels for 0%

profile of v1, /device:TPU:0, one launch (start us, length us, event | category | flops | bytes accessed | tf_op | source)
XLA Modules:
  0.0 1574.0 jit_solution(11822017238873283817)
XLA Ops:
  6.5 0.8 compare_select_fusion
  7.5 0.7 copy-done
  8.2 2.0 gather_fusion.1
  10.2 3.1 copy.60
  13.3 2.6 collective-permute-start.1
  16.0 1.5 collective-permute-start
  17.7 0.7 collective-permute-done
  18.4 0.6 gather_fusion
  19.2 4.5 pad_maximum_fusion
  23.7 2.9 gather_fusion.2
  26.6 1.2 fusion.32
  27.7 1.5 copy.61
  29.8 0.5 copy.63
  30.8 15.1 all_to_all.15
  46.2 6.2 stack.2
  52.4 34.4 %all-to-all-start.1 = ((bf16[128,2,8192]{2,1,0:T(2,128)(2,1)}), bf16[128,2,8192]{2,1,0:T(2,128)(2,1)}, u32[]{:S(2)}, u32[]{:S(2)}) async-start(bf16[128,2,8192]{2,1,0:T(2,128)(2,1)} %stack.2), calls=%async_computation.1 | async-start | bytes 8388608 | tf_op jit(solution)/shard_map/all_to_all | solution.py:129
  87.1 96.5 %all-to-all-done.1 = bf16[128,2,8192]{2,1,0:T(2,128)(2,1)} async-done(((bf16[128,2,8192]{2,1,0:T(2,128)(2,1)}), bf16[128,2,8192]{2,1,0:T(2,128)(2,1)}, u32[]{:S(2)}, u32[]{:S(2)}) %all-to-all-start.1) | async-done | bytes 4194336 | tf_op jit(solution)/shard_map/all_to_all | solution.py:129
  183.6 7.9 reshape_reshape.3
  191.4 6.8 copy.65
  198.3 3.2 gather_fusion.3
  201.5 2.1 fusion.1
  203.6 0.7 fusion.2
  204.3 2.7 fusion
  207.0 4.3 broadcast_in_dim.48
  211.3 10.3 scatter_fusion
  221.5 9.0 copy.66
  230.5 0.6 copy-done.16
  231.2 0.6 dynamic-slice
  232.4 1325.8 %all-reduce.3.cloned.1.call-done = f32[256,8192]{0,1:T(8,128)} async-done(((f32[256,8192]{0,1:T(8,128)}), f32[256,8192]{0,1:T(8,128)}) %all-reduce.3.cloned.1.call-update) | async-done | bytes 8388624
  1558.2 5.5 constant_dynamic-slice_fusion
  1563.6 2.8 copy.67
  1566.5 0.7 add_convert_fusion
  (58 shorter events, 2.0 us)
Async XLA Ops:
  6.5 1.6 copy-start
  8.1 7.8 copy-start.10
  8.1 9.3 copy-start.6
  8.1 9.3 copy-start.7
  8.1 9.4 copy-start.11
  8.2 9.4 copy-start.4
  13.3 5.8 collective-permute-start.1
  16.0 2.4 collective-permute-start
  27.7 18.2 %copy-start.3 = (bf16[2,8192]{1,0:T(2,128)(2,1)S(1)}, bf16[2,8192]{1,0:T(2,128)(2,1)}, u32[]{:S(2)}) copy-start(bf16[2,8192]{1,0:T(2,128)(2,1)} %param.24) | copy-start | bytes 98308
  27.7 18.4 %copy-start.5 = (f32[8192]{0:T(1024)S(1)}, f32[8192]{0:T(1024)}, u32[]{:S(2)}) copy-start(f32[8192]{0:T(1024)} %param.25) | copy-start | bytes 98308
  52.4 34.7 %copy-start.12 = (s32[1,32]{1,0:T(1,128)S(1)}, s32[1,32]{1,0:T(1,128)}, u32[]{:S(2)}) copy-start(s32[1,32]{1,0:T(1,128)} %param.28) | copy-start | bytes 388
  52.4 34.7 %copy-start.13 = (s32[1,32]{1,0:T(1,128)S(1)}, s32[1,32]{1,0:T(1,128)}, u32[]{:S(2)}) copy-start(s32[1,32]{1,0:T(1,128)} %param.32) | copy-start | bytes 388
  52.4 131.2 %all-to-all-start.1 = ((bf16[128,2,8192]{2,1,0:T(2,128)(2,1)}), bf16[128,2,8192]{2,1,0:T(2,128)(2,1)}, u32[]{:S(2)}, u32[]{:S(2)}) async-start(bf16[128,2,8192]{2,1,0:T(2,128)(2,1)} %stack.2), calls=%async_computation.1 | async-start | bytes 8388608 | tf_op jit(solution)/shard_map/all_to_all | solution.py:129
  86.8 1471.4 %all-reduce.3.cloned.1.call-start = ((), (), s32[]{:S(2)}) async-start(), calls=%async_computation.2 | async-start | bytes 16777216
  198.3 3.2 copy-start.14
  198.3 5.3 copy-start.15
  201.4 2.1 copy-start.9
  201.5 2.9 copy-start.2
  201.5 2.9 copy-start.8
  230.5 0.7 copy-start.16
  1558.2 9.0 copy-start.1
Sparse Core Ops, SparseCore 0:
  230.6 1327.4 all-reduce.2
